TPU v7x, 1024 devices: a whole 8x8x8 slice. The times are simulated.
1024 devices in a mesh: slab: 512 (over z, y, x), bal: 2 (over core).
Axes of the slice: x: 8, y: 8, z: 8, core: 2. Of those that a mesh axis runs over, the one named last changes fastest.
Arguments:
- order_parameter: float32 [512, 4, 32, 1024], P('slab', 'bal'), may hold values from -1 to 1
- concentration_excess: float32 [512, 4, 32, 1024], P('slab', 'bal'), may hold values from -1.8 to 1.8
- thermal_subcooling: float32 [512, 4, 32, 1024], P('slab', 'bal'), may hold values from -1.8 to 1.8
- holder_places_prior: int32 [512, 4], replicated, may hold values from 0 to 3, as said below
- holder_places_revised: int32 [512, 4], replicated, may hold values from 0 to 3, as said below
- update_flags: int32 [512, 4], replicated, may hold values 0 or 1
Outputs:
- phase_out: float32 [512, 4, 32, 1024], P('slab', 'bal')
- solute_out: float32 [512, 4, 32, 1024], P('slab', 'bal')
- temperature_out: float32 [512, 4, 32, 1024], P('slab', 'bal')
Inputs may be any that keep to these rules, and one draw needn't show every extreme that they name: `holder_places_prior`: each row is a permutation of the 4 positions of a layer; slot k belongs to the owner of index k // 2 along bal. `holder_places_revised`: each row is a permutation of the layer's positions. In every layer each owner gives exactly 1 of its blocks to other owners and receives exactly 1; every other block keeps its slot.
All inputs are finite; a program needn't handle non-finite values.
Results may differ from a plain program's by a relative error of at most 0.00002.
Values sent between devices are 32-bit elements; how exact they have to be, the bound alone decides.
A program may use at most 32 MiB of HBM per device.

v0:
```python
import jax
import jax.numpy as jnp
from jax import lax
from jax.sharding import PartitionSpec as P

TILE_SIDE_POINTS = 32
BZ = 4
BLK_DEV = 2
MOVE = 1


RATE = 0.1
ANISO = 0.05
COUPLE = 0.5
DIFF_SOLUTE = 0.08
DIFF_HEAT = 0.15
TINY = 0.0001


def with_halo(block, sides, width):
    for axis, dim in sides:
        count = lax.axis_size(axis)
        forward = [(i, i + 1) for i in range(count - 1)]
        backward = [(target, source) for source, target in forward]
        low = lax.ppermute(
            lax.slice_in_dim(block, block.shape[dim] - width, None, axis=dim), axis, forward
        )
        high = lax.ppermute(lax.slice_in_dim(block, 0, width, axis=dim), axis, backward)
        block = jnp.concatenate([low, block, high], axis=dim)
    return block


def in_one_piece(arrays, axis, dim, along):
    both = jnp.concatenate(arrays, axis=along)
    whole, at, outs = (lax.all_gather(both, axis, axis=dim, tiled=True), 0, [])
    for a in arrays:
        outs.append(lax.slice_in_dim(whole, at, at + a.shape[along], axis=along))
        at += a.shape[along]
    return tuple(outs)


def laplace(center, neighbours):
    return (
        neighbours[0]
        + neighbours[1]
        + (neighbours[2] + neighbours[3])
        + (neighbours[4] + neighbours[5])
        - 6.0 * center
    )


def march_forward(phase_now, solute_now, heat_now, near_phase, near_solute, near_heat, active_now):
    slope_x = 0.5 * (near_phase[0] - near_phase[1])
    slope_y = 0.5 * (near_phase[2] - near_phase[3])
    slope_z = 0.5 * (near_phase[4] - near_phase[5])
    sq_x = slope_x * slope_x
    sq_y = slope_y * slope_y
    sq_z = slope_z * slope_z
    slope_sq = sq_x + sq_y + sq_z
    quartic = sq_x * sq_x + sq_y * sq_y + sq_z * sq_z
    fourth_ratio = quartic / (slope_sq * slope_sq + TINY)
    anisotropy = 1.0 - 3.0 * ANISO + 4.0 * ANISO * fourth_ratio
    well_term = 1.0 - phase_now * phase_now
    forcing = (
        phase_now
        - phase_now * phase_now * phase_now
        - COUPLE * well_term * well_term * (solute_now + heat_now)
    )
    phase_new = phase_now + active_now * (
        RATE * (anisotropy * anisotropy * laplace(phase_now, near_phase) + forcing)
    )
    change = phase_new - phase_now
    solute_new = solute_now + DIFF_SOLUTE * laplace(solute_now, near_solute) + 0.5 * change
    heat_new = heat_now + DIFF_HEAT * laplace(heat_now, near_heat) + 0.5 * change
    return (phase_new, solute_new, heat_new)


def face_stack(quantities_bundle):
    stacks = []
    for quantity in quantities_bundle:
        blocks = quantity.shape[0]
        surfaces = [
            quantity[:, 0, :],
            quantity[:, -1, :],
            quantity[:, :, :TILE_SIDE_POINTS].reshape(blocks, -1),
            quantity[:, :, -TILE_SIDE_POINTS:].reshape(blocks, -1),
            quantity[:, :, 0::TILE_SIDE_POINTS].reshape(blocks, -1),
            quantity[:, :, TILE_SIDE_POINTS - 1 :: TILE_SIDE_POINTS].reshape(blocks, -1),
        ]
        stacks.append(jnp.stack(surfaces, axis=1))
    return jnp.stack(stacks, axis=2)


def halo_neighbours(center, border):
    blocks = center.shape[0]
    side = TILE_SIDE_POINTS
    x_padded = jnp.concatenate([border[0][:, None], center, border[1][:, None]], axis=1)
    y_padded = jnp.concatenate(
        [border[2].reshape(blocks, side, side), center, border[3].reshape(blocks, side, side)],
        axis=2,
    )
    x_upper = x_padded[:, 2:]
    x_lower = x_padded[:, :-2]
    y_upper = y_padded[:, :, 2 * side :]
    y_lower = y_padded[:, :, : side * side]
    z_index = lax.broadcasted_iota(jnp.int32, center.shape, 2) % side
    upper_face = jnp.broadcast_to(
        border[5].reshape(blocks, side, side, 1), (blocks, side, side, side)
    ).reshape(center.shape)
    lower_face = jnp.broadcast_to(
        border[4].reshape(blocks, side, side, 1), (blocks, side, side, side)
    ).reshape(center.shape)
    z_upper = jnp.where(z_index == side - 1, upper_face, jnp.roll(center, -1, axis=2))
    z_lower = jnp.where(z_index == 0, lower_face, jnp.roll(center, 1, axis=2))
    return (x_upper, x_lower, y_upper, y_lower, z_upper, z_lower)


def spread(own_faces):
    return lax.all_gather(own_faces, "bal", axis=0, tiled=True)


def ghosts(face_table, slot_lists, positions, own_faces, slab_at, slab_count):
    inverse_low, inverse_mid, inverse_high = slot_lists
    total = face_table.shape[0]
    rows_y = total // BZ
    block_row = positions // BZ
    block_col = positions % BZ
    y_lower = (block_row + rows_y - 1) % rows_y * BZ + block_col
    y_upper = (block_row + 1) % rows_y * BZ + block_col
    z_lower = block_row * BZ + (block_col + BZ - 1) % BZ
    z_upper = block_row * BZ + (block_col + 1) % BZ
    x_edges = jnp.take(face_table[:, 0:2], inverse_mid, axis=0)
    rim_faces = with_halo(x_edges, (("slab", 1),), 1)
    under_face = rim_faces[positions, 0]
    over_face = rim_faces[positions, 3]
    y_faces = (face_table[inverse_mid[y_lower], 3], face_table[inverse_mid[y_upper], 2])
    z_faces = (face_table[inverse_mid[z_lower], 5], face_table[inverse_mid[z_upper], 4])
    under_face = jnp.where(slab_at == 0, own_faces[:, 0], under_face)
    over_face = jnp.where(slab_at == slab_count - 1, own_faces[:, 1], over_face)
    return jnp.stack(
        [under_face, over_face, y_faces[0], y_faces[1], z_faces[0], z_faces[1]], axis=1
    )


def sweep(
    quantities_bundle, positions, own_faces, face_table, slot_lists, active_mid, slab_at, slab_count
):
    border = ghosts(face_table, slot_lists, positions, own_faces, slab_at, slab_count)
    active_now = active_mid[positions][:, None, None]
    near_sets = [
        halo_neighbours(
            quantities_bundle[index], tuple((border[:, side, index] for side in range(6)))
        )
        for index in range(3)
    ]
    return march_forward(
        quantities_bundle[0],
        quantities_bundle[1],
        quantities_bundle[2],
        near_sets[0],
        near_sets[1],
        near_sets[2],
        active_now,
    )


def layer_row(table, which, count):
    return lax.dynamic_slice_in_dim(table, jnp.clip(which, 0, count - 1), 1, 0)[0]


def inverse_of(perm):
    return jnp.argsort(perm)


def body(
    order_parameter,
    concentration_excess,
    thermal_subcooling,
    holder_places_prior,
    holder_places_revised,
    update_flags,
):
    slab_at = lax.axis_index("slab")
    slab_count = lax.axis_size("slab")
    bal_rank = lax.axis_index("bal")
    bal_count = lax.axis_size("bal")
    total = bal_count * BLK_DEV
    quantities_bundle = (order_parameter[0], concentration_excess[0], thermal_subcooling[0])
    active_mid = layer_row(update_flags, slab_at, slab_count).astype(jnp.float32)
    before_mid = layer_row(holder_places_prior, slab_at, slab_count)
    after_mid = layer_row(holder_places_revised, slab_at, slab_count)
    lists_before = tuple(
        (
            inverse_of(layer_row(holder_places_prior, slab_at + shift_by, slab_count))
            for shift_by in (-1, 0, 1)
        )
    )
    lists_after = tuple(
        (
            inverse_of(layer_row(holder_places_revised, slab_at + shift_by, slab_count))
            for shift_by in (-1, 0, 1)
        )
    )
    positions_before = lax.dynamic_slice_in_dim(before_mid, bal_rank * BLK_DEV, BLK_DEV)
    positions_after = lax.dynamic_slice_in_dim(after_mid, bal_rank * BLK_DEV, BLK_DEV)
    own_faces = face_stack(quantities_bundle)
    face_table = spread(own_faces)
    quantities_bundle = sweep(
        quantities_bundle,
        positions_before,
        own_faces,
        face_table,
        lists_before,
        active_mid,
        slab_at,
        slab_count,
    )
    owner_after = inverse_of(after_mid) // BLK_DEV
    slot_owner = jnp.arange(total, dtype=jnp.int32) // BLK_DEV
    leaving = (owner_after[before_mid] != slot_owner).astype(jnp.int32).reshape(bal_count, BLK_DEV)
    order = jnp.argsort(1 - leaving, axis=1, stable=True)[:, :MOVE]
    mover_slots = (jnp.arange(bal_count, dtype=jnp.int32)[:, None] * BLK_DEV + order).reshape(-1)
    mover_positions = before_mid[mover_slots]
    my_order = lax.dynamic_slice_in_dim(order, bal_rank, 1, 0)[0]
    outgoing = tuple((jnp.take(quantity, my_order, axis=0) for quantity in quantities_bundle))
    combined_positions = jnp.concatenate([positions_before, mover_positions], axis=0)
    chosen = jnp.argmax(combined_positions[None, :] == positions_after[:, None], axis=1)
    arrived = in_one_piece((outgoing[0], outgoing[1], outgoing[2]), "bal", 0, 1)
    quantities_bundle = tuple(
        (
            jnp.take(
                jnp.concatenate([quantities_bundle[index], arrived[index]], axis=0), chosen, axis=0
            )
            for index in range(3)
        )
    )
    own_faces = face_stack(quantities_bundle)
    face_table = spread(own_faces)
    quantities_bundle = sweep(
        quantities_bundle,
        positions_after,
        own_faces,
        face_table,
        lists_after,
        active_mid,
        slab_at,
        slab_count,
    )
    return (quantities_bundle[0][None], quantities_bundle[1][None], quantities_bundle[2][None])


def solution(mesh):
    placed = (
        P("slab", "bal", None, None),
        P("slab", "bal", None, None),
        P("slab", "bal", None, None),
        P(),
        P(),
        P(),
    )
    return jax.shard_map(
        body,
        mesh=mesh,
        in_specs=placed,
        out_specs=(
            P("slab", "bal", None, None),
            P("slab", "bal", None, None),
            P("slab", "bal", None, None),
        ),
        check_vma=False,
    )
```

profile of v0, /device:TPU:1, one launch (start us, length us, event | category | flops | bytes accessed | tf_op | source)
XLA Modules:
  0.0 130.8 jit_solution(17328898239661863314)
XLA Ops:
  0.6 0.9 fusion.128
  1.5 0.9 fusion.129
  2.5 1.3 slice.434
  3.8 1.3 slice.435
  6.6 0.9 dynamic-slice_reduce_fusion
  9.6 15.8 %all_gather.9 = f32[4,6,3,1024]{3,1,2,0:T(8,128)S(1)} all-gather(f32[2,6,3,1024]{3,1,2,0:T(8,128)S(1)} %pad_maximum_fusion.28), channel_id=1, replica_groups=mesh['slab'=512,'bal'=2] {'bal'}, dimensions={0}, use_global_device_ids=true | all-gather | bytes 442368 | tf_op jit(solution)/shard_map/all_gather | solution.py:119
  27.0 1.9 %collective-permute-start = (f32[4,1,3,1024]{3,1,2,0:T(1,128)}, f32[4,1,3,1024]{3,1,2,0:T(1,128)}, u32[]{:S(2)}, u32[]{:S(2)}) collective-permute-start(f32[4,1,3,1024]{3,1,2,0:T(1,128)} %get-tuple-element.122), channel_id=1, source_target_pairs={{0,2},{2,4},{4,6},{6,8},{8,10},{10,12},{12,14},{14,16},{16,18},{18... | collective-permute-start | bytes 147464 | tf_op jit(solution)/shard_map/ppermute | solution.py:25
  28.9 1.3 collective-permute-start.1
  31.1 0.9 fusion.122
  34.3 0.9 dynamic-slice_reduce_fusion.2
  48.1 0.9 convert_reduce_fusion
  64.6 1.1 broadcast_in_dim.158
  65.7 1.2 reshape.741
  67.6 1.1 broadcast_in_dim.160
  68.7 1.2 reshape.742
  73.3 1.0 pad_maximum_fusion.29
  76.1 1.1 broadcast_select_fusion.8
  80.3 2.5 %all_gather.10 = f32[2,96,1024]{2,1,0:T(8,128)S(1)} all-gather(f32[1,96,1024]{2,1,0:T(8,128)S(1)} %pad_maximum_fusion.3), channel_id=1, replica_groups=mesh['slab'=512,'bal'=2] {'bal'}, dimensions={0}, use_global_device_ids=true | all-gather | bytes 1179648 | tf_op jit(solution)/shard_map/all_gather | solution.py:35
  89.0 2.1 %all_gather.11 = f32[4,6,3,1024]{3,1,2,0:T(8,128)S(1)} all-gather(f32[2,6,3,1024]{3,1,2,0:T(8,128)S(1)} %pad_maximum_fusion.30), channel_id=1, replica_groups=mesh['slab'=512,'bal'=2] {'bal'}, dimensions={0}, use_global_device_ids=true | all-gather | bytes 442368 | tf_op jit(solution)/shard_map/all_gather | solution.py:119
  91.5 0.9 fusion.115
  95.2 0.9 gather_fusion.26
  97.0 5.0 %collective-permute-start.2 = (f32[4,1,3,1024]{3,1,2,0:T(1,128)}, f32[4,1,3,1024]{3,1,2,0:T(1,128)}, u32[]{:S(2)}, u32[]{:S(2)}) collective-permute-start(f32[4,1,3,1024]{3,1,2,0:T(1,128)} %get-tuple-element.120), channel_id=1, source_target_pairs={{0,2},{2,4},{4,6},{6,8},{8,10},{10,12},{12,14},{14,16},{16,18},{18... | collective-permute-start | bytes 147464 | tf_op jit(solution)/shard_map/ppermute | solution.py:25
  102.0 1.3 collective-permute-start.3
  112.7 1.4 %reshape_squeeze.54 = f32[2,32,32]{2,1,0:T(8,128)} reshape(f32[2,1024]{1,0:T(2,128)} %get-tuple-element.39) | data formatting | bytes 16384 | tf_op jit(solution)/shard_map/reshape;squeeze | solution.py:99
  116.8 1.1 broadcast_in_dim.167
  117.9 1.2 reshape.745
  119.8 1.1 broadcast_in_dim.169
  120.9 1.2 reshape.746
  123.5 1.0 pad_maximum_fusion.31
  126.3 1.1 broadcast_select_fusion.7
  128.3 1.4 %fusion.37 = (f32[1,2,32,1024]{3,2,1,0:T(8,128)}, f32[2,32,1024]{2,1,0:T(8,128)S(1)}) fusion(f32[2,32,1024]{2,1,0:T(8,128)S(1)} %get-tuple-element.150, f32[2,32,1024]{2,1,0:T(8,128)S(1)} %reshape.748, f32[2,32,1024]{2,1,0:T(8,128)S(1)} %reshape.747, f32[2,32,32]{2,1,0:T(8,128)S(1)} %copy-done.27, f32[2,32,32]{2,1,0:T(8,128)S(1)} %copy-done.26, ...), kind=kLoop, calls=%fused_computation.76 | loop fusion | flops 4784128 | bytes 3482632 | tf_op jit(solution)/shard_map/broadcast_in_dim | solution.py:249
  129.8 1.0 fusion.30
  (333 shorter events, 70.1 us)
Async XLA Ops:
  0.6 4.4 %copy-start.1 = (f32[1,2,32,1024]{3,2,1,0:T(8,128)S(1)}, f32[1,2,32,1024]{3,2,1,0:T(8,128)}, u32[]{:S(2)}) copy-start(f32[1,2,32,1024]{3,2,1,0:T(8,128)} %param.13) | copy-start | bytes 786436
  1.5 4.3 %copy-start.2 = (f32[1,2,32,1024]{3,2,1,0:T(8,128)S(1)}, f32[1,2,32,1024]{3,2,1,0:T(8,128)}, u32[]{:S(2)}) copy-start(f32[1,2,32,1024]{3,2,1,0:T(8,128)} %param.14) | copy-start | bytes 786436
  9.6 15.8 %copy-start.16 = (f32[2,6,3,1024]{3,1,2,0:T(8,128)}, f32[2,6,3,1024]{3,1,2,0:T(8,128)S(1)}, u32[]{:S(2)}) copy-start(f32[2,6,3,1024]{3,1,2,0:T(8,128)S(1)} %pad_maximum_fusion.28) | copy-start | bytes 442372
  27.0 46.3 %collective-permute-start = (f32[4,1,3,1024]{3,1,2,0:T(1,128)}, f32[4,1,3,1024]{3,1,2,0:T(1,128)}, u32[]{:S(2)}, u32[]{:S(2)}) collective-permute-start(f32[4,1,3,1024]{3,1,2,0:T(1,128)} %get-tuple-element.122), channel_id=1, source_target_pairs={{0,2},{2,4},{4,6},{6,8},{8,10},{10,12},{12,14},{14,16},{16,18},{18... | collective-permute-start | bytes 147464 | tf_op jit(solution)/shard_map/ppermute | solution.py:25
  28.9 44.4 %collective-permute-start.1 = (f32[4,1,3,1024]{3,1,2,0:T(1,128)}, f32[4,1,3,1024]{3,1,2,0:T(1,128)}, u32[]{:S(2)}, u32[]{:S(2)}) collective-permute-start(f32[4,1,3,1024]{3,1,2,0:T(1,128)} %get-tuple-element.123), channel_id=1, source_target_pairs={{2,0},{4,2},{6,4},{8,6},{10,8},{12,10},{14,12},{16,14},{18,16},{20... | collective-permute-start | bytes 147464 | tf_op jit(solution)/shard_map/ppermute | solution.py:28
  74.3 3.0 %copy-start.6 = (f32[2,32,1023]{2,1,0:T(8,128)S(1)}, f32[2,32,1023]{2,1,0:T(8,128)}, u32[]{:S(2)}) copy-start(f32[2,32,1023]{2,1,0:T(8,128)} %get-tuple-element.166) | copy-start | bytes 785668
  74.3 3.0 %copy-start.37 = (f32[2,32,1]{2,1,0:T(8,128)S(1)}, f32[2,32,1]{2,1,0:T(8,128)}, u32[]{:S(2)}) copy-start(f32[2,32,1]{2,1,0:T(8,128)} %get-tuple-element.167) | copy-start | bytes 772
  74.3 3.0 %copy-start.38 = (f32[2,32,1]{2,1,0:T(8,128)S(1)}, f32[2,32,1]{2,1,0:T(8,128)}, u32[]{:S(2)}) copy-start(f32[2,32,1]{2,1,0:T(8,128)} %get-tuple-element.168) | copy-start | bytes 772
  74.5 2.9 %copy-start.5 = (f32[2,32,1023]{2,1,0:T(8,128)S(1)}, f32[2,32,1023]{2,1,0:T(8,128)}, u32[]{:S(2)}) copy-start(f32[2,32,1023]{2,1,0:T(8,128)} %get-tuple-element.165) | copy-start | bytes 785668
  76.1 1.2 copy-start.35
  76.1 1.2 copy-start.36
  89.0 2.1 %copy-start.17 = (f32[2,6,3,1024]{3,1,2,0:T(8,128)}, f32[2,6,3,1024]{3,1,2,0:T(8,128)S(1)}, u32[]{:S(2)}) copy-start(f32[2,6,3,1024]{3,1,2,0:T(8,128)S(1)} %pad_maximum_fusion.30) | copy-start | bytes 442372
  96.2 7.7 %copy-start.55 = (s32[2]{0:T(128)S(1)}, s32[2]{0:T(128)}, u32[]{:S(2)}) copy-start(s32[2]{0:T(128)} %fusion.100) | copy-start | bytes 28
  96.9 6.3 %copy-start.57 = (s32[2]{0:T(128)S(1)}, s32[2]{0:T(128)}, u32[]{:S(2)}) copy-start(s32[2]{0:T(128)} %fusion.95) | copy-start | bytes 28
  97.0 26.5 %collective-permute-start.2 = (f32[4,1,3,1024]{3,1,2,0:T(1,128)}, f32[4,1,3,1024]{3,1,2,0:T(1,128)}, u32[]{:S(2)}, u32[]{:S(2)}) collective-permute-start(f32[4,1,3,1024]{3,1,2,0:T(1,128)} %get-tuple-element.120), channel_id=1, source_target_pairs={{0,2},{2,4},{4,6},{6,8},{8,10},{10,12},{12,14},{14,16},{16,18},{18... | collective-permute-start | bytes 147464 | tf_op jit(solution)/shard_map/ppermute | solution.py:25
  102.0 21.5 %collective-permute-start.3 = (f32[4,1,3,1024]{3,1,2,0:T(1,128)}, f32[4,1,3,1024]{3,1,2,0:T(1,128)}, u32[]{:S(2)}, u32[]{:S(2)}) collective-permute-start(f32[4,1,3,1024]{3,1,2,0:T(1,128)} %get-tuple-element.121), channel_id=1, source_target_pairs={{2,0},{4,2},{6,4},{8,6},{10,8},{12,10},{14,12},{16,14},{18,16},{20... | collective-permute-start | bytes 147464 | tf_op jit(solution)/shard_map/ppermute | solution.py:28
  112.7 1.4 %copy-start.47 = (f32[2,1024]{1,0:T(2,128)S(1)}, f32[2,1024]{1,0:T(2,128)}, u32[]{:S(2)}) copy-start(f32[2,1024]{1,0:T(2,128)} %get-tuple-element.42) | copy-start | bytes 24580
  120.9 1.2 copy-start.43
  124.5 1.2 copy-start.50
  124.5 3.0 %copy-start.4 = (f32[2,32,1023]{2,1,0:T(8,128)S(1)}, f32[2,32,1023]{2,1,0:T(8,128)}, u32[]{:S(2)}) copy-start(f32[2,32,1023]{2,1,0:T(8,128)} %get-tuple-element.79) | copy-start | bytes 785668
  124.5 3.0 %copy-start.33 = (f32[2,32,1]{2,1,0:T(8,128)S(1)}, f32[2,32,1]{2,1,0:T(8,128)}, u32[]{:S(2)}) copy-start(f32[2,32,1]{2,1,0:T(8,128)} %get-tuple-element.76) | copy-start | bytes 772
  124.5 3.0 %copy-start.34 = (f32[2,32,1]{2,1,0:T(8,128)S(1)}, f32[2,32,1]{2,1,0:T(8,128)}, u32[]{:S(2)}) copy-start(f32[2,32,1]{2,1,0:T(8,128)} %get-tuple-element.77) | copy-start | bytes 772
  124.7 2.9 %copy-start.3 = (f32[2,32,1023]{2,1,0:T(8,128)S(1)}, f32[2,32,1023]{2,1,0:T(8,128)}, u32[]{:S(2)}) copy-start(f32[2,32,1023]{2,1,0:T(8,128)} %get-tuple-element.78) | copy-start | bytes 785668
  126.3 1.2 copy-start.27
  126.3 1.2 copy-start.32
  128.2 1.5 %copy-start.9 = (f32[2,32,1024]{2,1,0:T(8,128)S(1)}, f32[2,32,1024]{2,1,0:T(8,128)}, u32[]{:S(2)}) copy-start(f32[2,32,1024]{2,1,0:T(8,128)} %reshape.745) | copy-start | bytes 786436
  128.2 1.5 %copy-start.10 = (f32[2,32,1024]{2,1,0:T(8,128)S(1)}, f32[2,32,1024]{2,1,0:T(8,128)}, u32[]{:S(2)}) copy-start(f32[2,32,1024]{2,1,0:T(8,128)} %reshape.746) | copy-start | bytes 786436
  128.2 1.5 %copy-start.14 = (f32[2,32,1023]{2,1,0:T(8,128)S(1)}, f32[2,32,1023]{2,1,0:T(8,128)}, u32[]{:S(2)}) copy-start(f32[2,32,1023]{2,1,0:T(8,128)} %get-tuple-element.70) | copy-start | bytes 785668
  128.3 1.5 %copy-start.15 = (f32[2,32,1023]{2,1,0:T(8,128)S(1)}, f32[2,32,1023]{2,1,0:T(8,128)}, u32[]{:S(2)}) copy-start(f32[2,32,1023]{2,1,0:T(8,128)} %get-tuple-element.71) | copy-start | bytes 785668
  128.3 1.5 %copy-start.25 = (f32[2,32,32]{2,1,0:T(8,128)S(1)}, f32[2,32,32]{2,1,0:T(8,128)}, u32[]{:S(2)}) copy-start(f32[2,32,32]{2,1,0:T(8,128)} %reshape_squeeze.57) | copy-start | bytes 24580
  128.3 1.5 %copy-start.30 = (f32[2,32,1]{2,1,0:T(8,128)S(1)}, f32[2,32,1]{2,1,0:T(8,128)}, u32[]{:S(2)}) copy-start(f32[2,32,1]{2,1,0:T(8,128)} %get-tuple-element.68) | copy-start | bytes 772
  128.3 1.5 %copy-start.31 = (f32[2,32,1]{2,1,0:T(8,128)S(1)}, f32[2,32,1]{2,1,0:T(8,128)}, u32[]{:S(2)}) copy-start(f32[2,32,1]{2,1,0:T(8,128)} %get-tuple-element.69) | copy-start | bytes 772
  (35 other events, 30.1 us)
where the time goes:
time: 133 us; the launch traced here: 131 us
  local copies, waits for them, and re-layouts  77.5 us (58%)
  blocking collectives  20.5 us (15%)
  other arithmetic  19.6 us (15%)
  starting transfers between devices  9.45 us (7%)
  between operations  3.83 us (3%)
    all_gather x2, blocking collectives, spread(): return lax.all_gather(own_faces, 'bal', axis=0, tiled=True)  17.9 us
    ppermute x2, starting transfers between devices, with_halo(): lax.ppermute(lax.slice_in_dim(block, block.shape[dim] - width, None, axis...  6.89 us
    unnamed x126, local copies, waits for them, and re-layouts  6.8 us
    broadcast_in_dim x12, local copies, waits for them, and re-layouts, halo_neighbours(): jnp.broadcast_to(border[4].reshape(blocks, side, side, 1), (blocks, side,...  5.24 us
    broadcast_in_dim x12, local copies, waits for them, and re-layouts, halo_neighbours(): jnp.broadcast_to(border[5].reshape(blocks, side, side, 1), (blocks, side,...  5.23 us
    slice x6, local copies, waits for them, and re-layouts, halo_neighbours(): z_lower = jnp.where(z_index == 0, lower_face, jnp.roll(center, 1, axis=2))  4.62 us
    reshape x6, local copies, waits for them, and re-layouts, halo_neighbours(): lower_face = jnp.broadcast_to(border[4].reshape(blocks, side, side, 1), (...  4.37 us
    reshape x6, local copies, waits for them, and re-layouts, halo_neighbours(): upper_face = jnp.broadcast_to(border[5].reshape(blocks, side, side, 1), (...  4.36 us
  transfers between devices with their start and end apart: 4, of which 0 were waited for; matrix products, arithmetic and copies ran while one was open for 44% of the time, Pallas kernels for 0%

commit v1 on v0

v1 whole, which is shorter than its diff:
```python
import functools

import jax
import jax.numpy as jnp
from jax import lax
from jax.experimental import pallas as pl
from jax.experimental.pallas import tpu as pltpu
from jax.sharding import PartitionSpec as P

RATE = 0.1
ANISO = 0.05
COUPLE = 0.5
DIFF_SOLUTE = 0.08
DIFF_HEAT = 0.15
TINY = 0.0001

MESH = pl.DeviceIdType.MESH
F32 = jnp.float32


def chunk_swap(planes, lane_block):
    turned = [planes[0]] + [pltpu.roll(planes[p], 32 * p, 1) for p in (1, 2, 3)]
    out = []
    for k in range(4):
        pick = [turned[(j - k) % 4] for j in range(4)]
        low = jnp.where(lane_block[0], pick[0], pick[1])
        high = jnp.where(lane_block[2], pick[2], pick[3])
        both = jnp.where(lane_block[1], low, high)
        out.append(both if k == 0 else pltpu.roll(both, 128 - 32 * k, 1))
    return out


def advance(center, below, above, active):
    def near(f, r):
        plane = center[f]
        y_upper = plane[r + 1] if r < 3 else pltpu.roll(plane[0], 7, 0)
        y_lower = plane[r - 1] if r > 0 else pltpu.roll(plane[3], 1, 0)
        z_upper = pltpu.roll(plane[r], 127, 1)
        z_lower = pltpu.roll(plane[r], 1, 1)
        return above[f][r], below[f][r], y_upper, y_lower, z_upper, z_lower

    def total(n):
        return ((n[0] + n[1]) + (n[2] + n[3])) + (n[4] + n[5])

    out = [[], [], []]
    for r in range(4):
        phase, solute, heat = center[0][r], center[1][r], center[2][r]
        n = near(0, r)
        dx, dy, dz = n[0] - n[1], n[2] - n[3], n[4] - n[5]
        qx, qy, qz = dx * dx, dy * dy, dz * dz
        slope_sq = qx + qy + qz
        quartic = qx * qx + qy * qy + qz * qz
        ratio = quartic / (slope_sq * slope_sq + 16.0 * TINY)
        aniso = (1.0 - 3.0 * ANISO) + 4.0 * ANISO * ratio
        well = 1.0 - phase * phase
        forcing = phase * well - (COUPLE * (well * well)) * (solute + heat)
        change = active * (aniso * aniso * (total(n) - 6.0 * phase) + forcing)
        half = 0.5 * change
        out[0].append(phase + change)
        out[1].append(solute + DIFF_SOLUTE * (total(near(1, r)) - 6.0 * solute) + half)
        out[2].append(heat + DIFF_HEAT * (total(near(2, r)) - 6.0 * heat) + half)
    return out


def kernel(
    slabs,
    p_in,
    u_in,
    h_in,
    prior_in,
    revised_in,
    flags_in,
    p_out,
    u_out,
    h_out,
    main,
    extra,
    halo,
    first,
    second,
    final,
    leaving,
    prior,
    revised,
    flags,
    table_sem,
    local_sem,
    chip_send,
    chip_recv,
    side_send,
    side_recv,
    back_send,
    back_recv,
):
    fields = (p_in, u_in, h_in)
    outs = (p_out, u_out, h_out)
    s = lax.axis_index("slab")
    b = lax.axis_index("bal")
    ob = 1 - b
    last = slabs - 1
    has_low, has_high = s > 0, s < last
    barrier = pltpu.get_barrier_semaphore()

    pl.semaphore_signal(barrier, inc=1, device_id=(s, ob), device_id_type=MESH)

    @pl.when((b == 0) & has_low)
    def _():
        for k in range(2):
            pl.semaphore_signal(barrier, inc=1, device_id=(s - 1, k), device_id_type=MESH)

    @pl.when((b == 1) & has_high)
    def _():
        for k in range(2):
            pl.semaphore_signal(barrier, inc=1, device_id=(s + 1, k), device_id_type=MESH)

    tables = [
        pltpu.make_async_copy(src, dst, table_sem.at[i])
        for i, (src, dst) in enumerate(
            ((prior_in, prior), (revised_in, revised), (flags_in, flags))
        )
    ]
    for t in tables:
        t.start()
    pl.semaphore_wait(barrier, 1 + jnp.where(has_low, 1, 0) + jnp.where(has_high, 1, 0))

    def other_core(src, dst, i):
        return pltpu.make_async_remote_copy(
            src, dst, chip_send.at[i], chip_recv.at[i], device_id=(s, ob), device_id_type=MESH
        )

    mine = pl.ds(2 * b, 2)
    theirs = pl.ds(2 * ob, 2)

    def edge_row(core, j):
        return 2 - core, jnp.where(core == 1, 6 + j, 1 - j)

    for f in range(3):
        for j in range(2):
            t, i = edge_row(ob, j)
            other_core(fields[f].at[:, t, :, i], extra.at[f, j, mine], 1).start()
        for c in range(8):
            other_core(fields[f].at[:, theirs, c], main.at[f, mine, :, :, c], 0).start()

    def to_layer(side, target):
        for f in range(3):
            for j in range(2):
                src = fields[f].at[:, 3, :, 7 - j] if side == 0 else fields[f].at[:, 0, :, j]
                pltpu.make_async_remote_copy(
                    src,
                    halo.at[b, f, j],
                    side_send.at[side],
                    side_recv,
                    device_id=(target, side),
                    device_id_type=MESH,
                ).start()

    @pl.when(has_high)
    def _():
        to_layer(0, s + 1)

    @pl.when(has_low)
    def _():
        to_layer(1, s - 1)

    for f in range(3):
        for j in range(2):
            t, i = edge_row(b, j)
            pltpu.make_async_copy(
                fields[f].at[:, t, :, i], extra.at[f, j, mine], local_sem.at[1]
            ).start()
        for c in range(8):
            pltpu.make_async_copy(
                fields[f].at[:, mine, c], main.at[f, mine, :, :, c], local_sem.at[0]
            ).start()

    for t in tables:
        t.wait()
    next_to = jnp.where(b == 0, jnp.where(has_low, s - 1, s), jnp.where(has_high, s + 1, s))
    at_wall = ((b == 0) & (s == 0)) | ((b == 1) & (s == last))

    def slots_of(table, row):
        held = [table[k, row] for k in range(4)]
        return [
            jnp.where(held[1] == p, 1, jnp.where(held[2] == p, 2, jnp.where(held[3] == p, 3, 0)))
            for p in range(4)
        ]

    slot_here = slots_of(prior, s)
    slot_next = slots_of(prior, next_to)
    place_mine = [revised[2 * b + k, s] for k in range(2)]
    place_theirs = [revised[2 * ob + k, s] for k in range(2)]
    lane = lax.broadcasted_iota(jnp.int32, (8, 128), 1)
    lane_block = [lane < 32, lane < 64, lane < 96]

    def activity(row):
        a = [RATE * flags[p, row].astype(F32) for p in range(4)]
        low = jnp.where(lane_block[0], a[0], a[1])
        high = jnp.where(lane_block[2], a[2], a[3])
        return jnp.where(lane_block[1], low, high)

    active_here = activity(s)
    active_next = activity(next_to)

    def row_of(u):
        return jnp.where(b == 1, u - 2, 17 - u)

    def keep(u, planes, f):
        for r in range(4):
            first[f, u, r] = planes[r]

    def gather_extra(j):
        for f in range(3):
            keep(j, chunk_swap([extra[f, j, slot_here[p]] for p in range(4)], lane_block), f)

    def gather(u):
        row = row_of(u)
        for f in range(3):
            planes = [main[f, slot_here[p], row // 8, row % 8] for p in range(4)]
            keep(u, chunk_swap(planes, lane_block), f)

    def gather_halo(j):
        for f in range(3):
            planes = chunk_swap(
                [halo[slot_next[p] // 2, f, j, slot_next[p] % 2] for p in range(4)], lane_block
            )
            keep(18 + j, [jnp.where(at_wall, first[f, 17, r], planes[r]) for r in range(4)], f)

    def rows(src, u):
        return [[src[f, u, r] for r in range(4)] for f in range(3)]

    def step_one(u, active):
        new = advance(rows(first, u), rows(first, u - 1), rows(first, u + 1), active)
        for f in range(3):
            for r in range(4):
                second[f, u, r] = new[f][r]
        return new

    def step_two(u):
        new = advance(rows(second, u), rows(second, u - 1), rows(second, u + 1), active_here)
        for f in range(3):
            planes = chunk_swap(new[f], lane_block)
            for p in range(4):
                final[f, p, u - 2] = planes[p]

    def deal(u):
        row = row_of(u)
        for f in range(3):
            for k in range(2):
                leaving[f, k, row // 8, row % 8] = final[f, place_theirs[k], u - 2]
                outs[f][k, 2 * b + row // 8, row % 8] = final[f, place_mine[k], u - 2]

    pltpu.make_async_copy(main.at[:, mine], main.at[:, mine], local_sem.at[0]).wait()
    pltpu.make_async_copy(extra.at[:, :, mine], extra.at[:, :, mine], local_sem.at[1]).wait()
    other_core(main.at[:, mine], main.at[:, theirs], 0).wait_recv()
    other_core(extra.at[:, :, mine], extra.at[:, :, theirs], 1).wait_recv()

    gather_extra(0)
    gather_extra(1)
    gather(2)
    step_one(1, active_here)
    gather(3)
    step_one(2, active_here)
    gather(4)
    step_one(3, active_here)
    gather(5)

    def stage(t, carry):
        step_two(t - 4)
        step_one(t - 2, active_here)
        gather(t)
        return carry

    lax.fori_loop(6, 18, stage, 0)
    step_two(14)
    step_one(16, active_here)
    step_two(15)

    def side_copy(side, ref):
        return pltpu.make_async_remote_copy(
            ref, ref, side_send.at[side], side_recv, device_id=(s, ob), device_id_type=MESH
        )

    @pl.when(jnp.logical_not(at_wall))
    def _():
        side_copy(0, halo).wait_recv()

    gather_halo(0)
    gather_halo(1)
    step_one(17, active_here)
    beside = step_one(18, active_next)
    for f in range(3):
        for r in range(4):
            second[f, 18, r] = jnp.where(at_wall, second[f, 17, r], beside[f][r])
    step_two(16)
    step_two(17)

    def deal_all(t, carry):
        for i in range(4):
            deal(2 + 4 * t + i)
        return carry

    lax.fori_loop(0, 4, deal_all, 0)

    def back(f):
        return pltpu.make_async_remote_copy(
            leaving.at[f],
            outs[f].at[:, pl.ds(2 * b, 2)],
            back_send.at[f],
            back_recv.at[f],
            device_id=(s, ob),
            device_id_type=MESH,
        )

    for f in range(3):
        back(f).start()
    other_core(main.at[:, mine], main.at[:, theirs], 0).wait_send()
    other_core(extra.at[:, :, mine], extra.at[:, :, theirs], 1).wait_send()

    @pl.when(has_high)
    def _():
        side_copy(0, halo.at[b]).wait_send()

    @pl.when(has_low)
    def _():
        side_copy(1, halo.at[b]).wait_send()

    for f in range(3):
        back(f).wait()


def deliver(p_in, u_in, h_in, p_out, u_out, h_out, sem):
    copies = []
    for f, (src, dst) in enumerate(((p_in, p_out), (u_in, u_out), (h_in, h_out))):
        for c in range(8):
            copies.append(
                pltpu.make_async_copy(src.at[:, :, :, c], dst.at[:, :, c], sem.at[f, c])
            )
    for copy in copies:
        copy.start()
    for copy in copies:
        copy.wait()


def body(slabs, p, u, h, prior, revised, flags):
    tiles = [a.reshape(2, 4, 8, 8, 128).transpose(0, 1, 3, 2, 4) for a in (p, u, h)]
    block = jax.ShapeDtypeStruct((2, 4, 8, 8, 128), F32)
    anywhere = pl.BlockSpec(memory_space=pl.ANY)
    hbm = pl.BlockSpec(memory_space=pltpu.HBM)
    vmem = pl.BlockSpec(memory_space=pltpu.VMEM)
    dma = pltpu.SemaphoreType.DMA
    table = pltpu.SMEM((4, slabs), jnp.int32)
    done = pl.pallas_call(
        functools.partial(kernel, slabs),
        out_shape=(block,) * 3,
        in_specs=[hbm] * 6,
        out_specs=(vmem,) * 3,
        scratch_shapes=[
            pltpu.VMEM((3, 4, 2, 8, 8, 128), F32),
            pltpu.VMEM((3, 2, 4, 8, 128), F32),
            pltpu.VMEM((2, 3, 2, 2, 8, 128), F32),
            pltpu.VMEM((3, 20, 4, 8, 128), F32),
            pltpu.VMEM((3, 20, 4, 8, 128), F32),
            pltpu.VMEM((3, 4, 16, 8, 128), F32),
            pltpu.VMEM((3, 2, 2, 8, 8, 128), F32),
            table,
            table,
            table,
            dma((3,)),
            dma((2,)),
            dma((2,)),
            dma((2,)),
            dma((2,)),
            dma,
            dma((3,)),
            dma((3,)),
        ],
        compiler_params=pltpu.CompilerParams(
            collective_id=0, has_side_effects=True, vmem_limit_bytes=16 << 20
        ),
        name="sweeps",
    )(*(pltpu.with_memory_space_constraint(a, pltpu.HBM) for a in (*tiles, prior.T, revised.T, flags.T)))
    placed = pl.pallas_call(
        deliver,
        out_shape=(block,) * 3,
        in_specs=[anywhere] * 3,
        out_specs=(anywhere,) * 3,
        scratch_shapes=[dma((3, 8))],
        compiler_params=pltpu.CompilerParams(vmem_limit_bytes=4 << 20),
        name="deliver",
    )(*done)
    return tuple(a.transpose(0, 1, 3, 2, 4).reshape(1, 2, 32, 1024) for a in placed)


def solution(mesh):
    blocks = P("slab", "bal", None, None)
    return jax.shard_map(
        functools.partial(body, mesh.shape["slab"]),
        mesh=mesh,
        in_specs=(blocks,) * 3 + (P(),) * 3,
        out_specs=(blocks,) * 3,
        check_vma=False,
    )
```

time: 133 us -> 24.3 us (0.18); the launches traced: 131 us -> 24 us
  local copies, waits for them, and re-layouts: 77.5 us -> 0 us
  Pallas kernels: 0 us -> 23.4 us
  blocking collectives: 20.5 us -> 0 us
  other arithmetic: 19.6 us -> 0 us
  starting transfers between devices: 9.45 us -> 0 us
  between operations: 3.83 us -> 0.64 us
    pallas_call x0 -> x2, Pallas kernels: none -> 23.4 us  [the longest x1 22.3 us: body(): pl.pallas_call(functools.partial(kernel, slabs), out_shape=(block,) * 3,...]
    slice x47 -> x0, local copies, waits for them, and re-layouts: 20.9 us -> none  [the longest x6 4.62 us: halo_neighbours(): z_lower = jnp.where(z_index == 0, lower_face, jnp.roll(center, 1, axis=2))]
    all_gather x3 -> x0, blocking collectives: 20.5 us -> none  [the longest x2 17.9 us: spread(): return lax.all_gather(own_faces, 'bal', axis=0, tiled=True)]
    gather x29 -> x0, local copies, waits for them, and re-layouts: 17.1 us -> none  [the longest x3 2.06 us: body(): jnp.take(jnp.concatenate([quantities_bundle[index], arrived[index]], axis...]
    broadcast_in_dim x24 -> x0, local copies, waits for them, and re-layouts: 10.5 us -> none  [the longest x12 5.24 us: halo_neighbours(): jnp.broadcast_to(border[4].reshape(blocks, side, side, 1), (blocks, side,...]
    another operation x46 -> x0, local copies, waits for them, and re-layouts: 10.2 us -> none  [the longest x6 4.1 us: halo_neighbours(): border[2].reshape(blocks, side, side)]
    ppermute x4 -> x0, starting transfers between devices: 9.45 us -> none  [the longest x2 6.89 us: with_halo(): lax.ppermute(lax.slice_in_dim(block, block.shape[dim] - width, None, axis...]
    reshape x12 -> x0, local copies, waits for them, and re-layouts: 8.73 us -> none  [the longest x6 4.37 us: halo_neighbours(): lower_face = jnp.broadcast_to(border[4].reshape(blocks, side, side, 1), (...]
  transfers between devices with their start and end apart: 4 -> 0, of which waited for: 0 -> 0; matrix products, arithmetic and copies ran while one was open for 44% -> 0% of each run, Pallas kernels for 0% -> 0%
where the time goes in v1:
time: 24.3 us; the launch traced here: 24 us
  Pallas kernels  23.4 us (96%)
  between operations  0.64 us (3%)
    pallas_call x1, Pallas kernels, body(): pl.pallas_call(functools.partial(kernel, slabs), out_shape=(block,) * 3,...  22.3 us
    pallas_call x1, Pallas kernels, body(): pl.pallas_call(deliver, out_shape=(block,) * 3, in_specs=[anywhere] * 3,...  1.08 us

profile of v1, /device:TPU:1, one launch (start us, length us, event | category | flops | bytes accessed | tf_op | source)
XLA Modules:
  0.0 24.0 jit_solution(1816127905579286229)
XLA Ops:
  0.6 22.3 %sweeps.1 = (f32[2,4,8,8,128]{4,3,2,1,0:T(8,128)S(1)}, f32[2,4,8,8,128]{4,3,2,1,0:T(8,128)S(1)}, f32[2,4,8,8,128]{4,3,2,1,0:T(8,128)S(1)}) custom-call(f32[2,4,8,8,128]{4,3,2,1,0:T(8,128)} %bitcast.21, f32[2,4,8,8,128]{4,3,2,1,0:T(8,128)} %bitcast.22, f32[2,4,8,8,128]{4,3,2,1,0:T(8,128)} %bitcast.23, s32[4,512]{1,0:T(4,128)} %bitcast.24, s32[4,512]{1,0:T(4,128)} %bitcast.25, ...), custom_call_target="tpu_custom_call" | custom-call | tf_op jit(solution)/shard_map/sweeps/pallas_call | solution.py:352
  22.9 1.1 %deliver.1 = (f32[2,4,8,8,128]{4,3,2,1,0:T(8,128)}, f32[2,4,8,8,128]{4,3,2,1,0:T(8,128)}, f32[2,4,8,8,128]{4,3,2,1,0:T(8,128)}) custom-call(f32[2,4,8,8,128]{4,3,2,1,0:T(8,128)S(1)} %get-tuple-element.9.p_in, f32[2,4,8,8,128]{4,3,2,1,0:T(8,128)S(1)} %get-tuple-element.10.u_in, f32[2,4,8,8,128]{4,3,2,1,0:T(8,128)S(1)} %get-tuple-element.11.h_in), custom_call_target="tpu_custom_call" | custom-call | tf_op jit(solution)/shard_map/deliver/pallas_call | solution.py:382

commit v2 on v1

--- a/solution.py
+++ b/solution.py
@@ -31,34 +31,31 @@
 
 
 def advance(center, below, above, active):
-    def near(f, r):
+    def total(f, r):
         plane = center[f]
         y_upper = plane[r + 1] if r < 3 else pltpu.roll(plane[0], 7, 0)
         y_lower = plane[r - 1] if r > 0 else pltpu.roll(plane[3], 1, 0)
-        z_upper = pltpu.roll(plane[r], 127, 1)
-        z_lower = pltpu.roll(plane[r], 1, 1)
-        return above[f][r], below[f][r], y_upper, y_lower, z_upper, z_lower
-
-    def total(n):
-        return ((n[0] + n[1]) + (n[2] + n[3])) + (n[4] + n[5])
+        z_upper, z_lower = pltpu.roll(plane[r], 127, 1), pltpu.roll(plane[r], 1, 1)
+        around = ((above[f][r] + below[f][r]) + (y_upper + y_lower)) + (z_upper + z_lower)
+        return around, y_upper - y_lower, z_upper - z_lower
 
     out = [[], [], []]
     for r in range(4):
         phase, solute, heat = center[0][r], center[1][r], center[2][r]
-        n = near(0, r)
-        dx, dy, dz = n[0] - n[1], n[2] - n[3], n[4] - n[5]
+        around, dy, dz = total(0, r)
+        dx = above[0][r] - below[0][r]
         qx, qy, qz = dx * dx, dy * dy, dz * dz
         slope_sq = qx + qy + qz
         quartic = qx * qx + qy * qy + qz * qz
         ratio = quartic / (slope_sq * slope_sq + 16.0 * TINY)
         aniso = (1.0 - 3.0 * ANISO) + 4.0 * ANISO * ratio
         well = 1.0 - phase * phase
-        forcing = phase * well - (COUPLE * (well * well)) * (solute + heat)
-        change = active * (aniso * aniso * (total(n) - 6.0 * phase) + forcing)
+        forcing = well * (phase - (COUPLE * well) * (solute + heat))
+        change = active * (aniso * aniso * (around - 6.0 * phase) + forcing)
         half = 0.5 * change
         out[0].append(phase + change)
-        out[1].append(solute + DIFF_SOLUTE * (total(near(1, r)) - 6.0 * solute) + half)
-        out[2].append(heat + DIFF_HEAT * (total(near(2, r)) - 6.0 * heat) + half)
+        for f, rate, here in ((1, DIFF_SOLUTE, solute), (2, DIFF_HEAT, heat)):
+            out[f].append(((1.0 - 6.0 * rate) * here + rate * total(f, r)[0]) + half)
     return out
 
 
@@ -201,8 +198,8 @@
     active_here = activity(s)
     active_next = activity(next_to)
 
-    def row_of(u):
-        return jnp.where(b == 1, u - 2, 17 - u)
+    def place(t, i):
+        return jnp.where(b == 1, t, 1 - t), jnp.where(b == 1, i, 7 - i)
 
     def keep(u, planes, f):
         for r in range(4):
@@ -212,11 +209,11 @@
         for f in range(3):
             keep(j, chunk_swap([extra[f, j, slot_here[p]] for p in range(4)], lane_block), f)
 
-    def gather(u):
-        row = row_of(u)
-        for f in range(3):
-            planes = [main[f, slot_here[p], row // 8, row % 8] for p in range(4)]
-            keep(u, chunk_swap(planes, lane_block), f)
+    def gather(t, i):
+        tile, row = place(t, i)
+        for f in range(3):
+            planes = [main[f, slot_here[p], tile, row] for p in range(4)]
+            keep(2 + 8 * t + i, chunk_swap(planes, lane_block), f)
 
     def gather_halo(j):
         for f in range(3):
@@ -228,12 +225,12 @@
     def rows(src, u):
         return [[src[f, u, r] for r in range(4)] for f in range(3)]
 
-    def step_one(u, active):
+    def step_one(u):
+        active = jnp.where(u == 18, active_next, active_here)
         new = advance(rows(first, u), rows(first, u - 1), rows(first, u + 1), active)
         for f in range(3):
             for r in range(4):
                 second[f, u, r] = new[f][r]
-        return new
 
     def step_two(u):
         new = advance(rows(second, u), rows(second, u - 1), rows(second, u + 1), active_here)
@@ -242,77 +239,70 @@
             for p in range(4):
                 final[f, p, u - 2] = planes[p]
 
-    def deal(u):
-        row = row_of(u)
+    def deal(t, i):
+        tile, row = place(t, i)
         for f in range(3):
             for k in range(2):
-                leaving[f, k, row // 8, row % 8] = final[f, place_theirs[k], u - 2]
-                outs[f][k, 2 * b + row // 8, row % 8] = final[f, place_mine[k], u - 2]
-
-    pltpu.make_async_copy(main.at[:, mine], main.at[:, mine], local_sem.at[0]).wait()
-    pltpu.make_async_copy(extra.at[:, :, mine], extra.at[:, :, mine], local_sem.at[1]).wait()
-    other_core(main.at[:, mine], main.at[:, theirs], 0).wait_recv()
-    other_core(extra.at[:, :, mine], extra.at[:, :, theirs], 1).wait_recv()
-
-    gather_extra(0)
-    gather_extra(1)
-    gather(2)
-    step_one(1, active_here)
-    gather(3)
-    step_one(2, active_here)
-    gather(4)
-    step_one(3, active_here)
-    gather(5)
-
-    def stage(t, carry):
-        step_two(t - 4)
-        step_one(t - 2, active_here)
-        gather(t)
-        return carry
-
-    lax.fori_loop(6, 18, stage, 0)
-    step_two(14)
-    step_one(16, active_here)
-    step_two(15)
+                leaving[f, k, tile, row] = final[f, place_theirs[k], 8 * t + i]
+                outs[f][k, 2 * b + tile, row] = final[f, place_mine[k], 8 * t + i]
+
+    def back(f, t, h):
+        tile, row = jnp.where(b == 1, t, 1 - t), jnp.where(b == 1, 4 * h, 4 - 4 * h)
+        return pltpu.make_async_remote_copy(
+            leaving.at[f, :, tile, pl.ds(row, 4)],
+            outs[f].at[:, 2 * b + tile, pl.ds(row, 4)],
+            back_send.at[2 * t + h, f],
+            back_recv.at[2 * t + h, f],
+            device_id=(s, ob),
+            device_id_type=MESH,
+        )
 
     def side_copy(side, ref):
         return pltpu.make_async_remote_copy(
             ref, ref, side_send.at[side], side_recv, device_id=(s, ob), device_id_type=MESH
         )
 
+    pltpu.make_async_copy(main.at[:, mine], main.at[:, mine], local_sem.at[0]).wait()
+    pltpu.make_async_copy(extra.at[:, :, mine], extra.at[:, :, mine], local_sem.at[1]).wait()
+    other_core(extra.at[:, :, mine], extra.at[:, :, theirs], 1).wait_recv()
+    other_core(main.at[:, mine], main.at[:, theirs], 0).wait_recv()
+    def gather_tile(t, carry):
+        for i in range(8):
+            gather(t, i)
+        return carry
+
+    lax.fori_loop(0, 2, gather_tile, 0)
+    for j in range(2):
+        gather_extra(j)
+
     @pl.when(jnp.logical_not(at_wall))
     def _():
         side_copy(0, halo).wait_recv()
 
-    gather_halo(0)
-    gather_halo(1)
-    step_one(17, active_here)
-    beside = step_one(18, active_next)
+    for j in range(2):
+        gather_halo(j)
+    def step_rows(n, carry):
+        for i in range(6):
+            step_one(1 + 6 * n + i)
+        return carry
+
+    lax.fori_loop(0, 3, step_rows, 0)
     for f in range(3):
         for r in range(4):
-            second[f, 18, r] = jnp.where(at_wall, second[f, 17, r], beside[f][r])
-    step_two(16)
-    step_two(17)
-
-    def deal_all(t, carry):
+            second[f, 18, r] = jnp.where(at_wall, second[f, 17, r], second[f, 18, r])
+
+    def finish(n, carry):
+        t, h = n // 2, n % 2
         for i in range(4):
-            deal(2 + 4 * t + i)
+            step_two(2 + 4 * n + i)
+        for i in range(4):
+            deal(t, 4 * h + i)
+        for f in range(3):
+            back(f, t, h).start()
         return carry
 
-    lax.fori_loop(0, 4, deal_all, 0)
-
-    def back(f):
-        return pltpu.make_async_remote_copy(
-            leaving.at[f],
-            outs[f].at[:, pl.ds(2 * b, 2)],
-            back_send.at[f],
-            back_recv.at[f],
-            device_id=(s, ob),
-            device_id_type=MESH,
-        )
-
-    for f in range(3):
-        back(f).start()
+    lax.fori_loop(0, 4, finish, 0)
+
     other_core(main.at[:, mine], main.at[:, theirs], 0).wait_send()
     other_core(extra.at[:, :, mine], extra.at[:, :, theirs], 1).wait_send()
 
@@ -324,21 +314,18 @@
     def _():
         side_copy(1, halo.at[b]).wait_send()
 
-    for f in range(3):
-        back(f).wait()
+    for n in range(4):
+        for f in range(3):
+            back(f, n // 2, n % 2).wait()
 
 
 def deliver(p_in, u_in, h_in, p_out, u_out, h_out, sem):
-    copies = []
-    for f, (src, dst) in enumerate(((p_in, p_out), (u_in, u_out), (h_in, h_out))):
+    pairs = ((p_in, p_out), (u_in, u_out), (h_in, h_out))
+    for f, (src, dst) in enumerate(pairs):
         for c in range(8):
-            copies.append(
-                pltpu.make_async_copy(src.at[:, :, :, c], dst.at[:, :, c], sem.at[f, c])
-            )
-    for copy in copies:
-        copy.start()
-    for copy in copies:
-        copy.wait()
+            pltpu.make_async_copy(src.at[:, :, :, c], dst.at[:, :, c], sem.at[f]).start()
+    for f, (src, dst) in enumerate(pairs):
+        pltpu.make_async_copy(src, dst, sem.at[f]).wait()
 
 
 def body(slabs, p, u, h, prior, revised, flags):
@@ -371,8 +358,8 @@
             dma((2,)),
             dma((2,)),
             dma,
-            dma((3,)),
-            dma((3,)),
+            dma((4, 3)),
+            dma((4, 3)),
         ],
         compiler_params=pltpu.CompilerParams(
             collective_id=0, has_side_effects=True, vmem_limit_bytes=16 << 20
@@ -384,7 +371,7 @@
         out_shape=(block,) * 3,
         in_specs=[anywhere] * 3,
         out_specs=(anywhere,) * 3,
-        scratch_shapes=[dma((3, 8))],
+        scratch_shapes=[dma((3,))],
         compiler_params=pltpu.CompilerParams(vmem_limit_bytes=4 << 20),
         name="deliver",
     )(*done)

time: 24.3 us -> 22.9 us (0.942)
  Pallas kernels: 23.4 us -> 22 us
    pallas_call x1, Pallas kernels: 22.3 us -> 21.1 us  [body(): pl.pallas_call(functools.partial(kernel, slabs), out_shape=(block,) * 3,...]
where the time goes in v2:
time: 22.9 us; the launch traced here: 22.7 us
  Pallas kernels  22 us (96%)
  between operations  0.64 us (3%)
    pallas_call x1, Pallas kernels, body(): pl.pallas_call(functools.partial(kernel, slabs), out_shape=(block,) * 3,...  21.1 us
    pallas_call x1, Pallas kernels, body(): pl.pallas_call(deliver, out_shape=(block,) * 3, in_specs=[anywhere] * 3,...  0.89 us

profile of v2, /device:TPU:1, one launch (start us, length us, event | category | flops | bytes accessed | tf_op | source)
XLA Modules:
  0.0 22.7 jit_solution(10157350006215066524)
XLA Ops:
  0.6 21.1 %sweeps.1 = (f32[2,4,8,8,128]{4,3,2,1,0:T(8,128)S(1)}, f32[2,4,8,8,128]{4,3,2,1,0:T(8,128)S(1)}, f32[2,4,8,8,128]{4,3,2,1,0:T(8,128)S(1)}) custom-call(f32[2,4,8,8,128]{4,3,2,1,0:T(8,128)} %bitcast.21, f32[2,4,8,8,128]{4,3,2,1,0:T(8,128)} %bitcast.22, f32[2,4,8,8,128]{4,3,2,1,0:T(8,128)} %bitcast.23, s32[4,512]{1,0:T(4,128)} %bitcast.24, s32[4,512]{1,0:T(4,128)} %bitcast.25, ...), custom_call_target="tpu_custom_call" | custom-call | tf_op jit(solution)/shard_map/sweeps/pallas_call | solution.py:339
  21.8 0.9 %deliver.1 = (f32[2,4,8,8,128]{4,3,2,1,0:T(8,128)}, f32[2,4,8,8,128]{4,3,2,1,0:T(8,128)}, f32[2,4,8,8,128]{4,3,2,1,0:T(8,128)}) custom-call(f32[2,4,8,8,128]{4,3,2,1,0:T(8,128)S(1)} %get-tuple-element.9.p_in, f32[2,4,8,8,128]{4,3,2,1,0:T(8,128)S(1)} %get-tuple-element.10.u_in, f32[2,4,8,8,128]{4,3,2,1,0:T(8,128)S(1)} %get-tuple-element.11.h_in), custom_call_target="tpu_custom_call" | custom-call | tf_op jit(solution)/shard_map/deliver/pallas_call | solution.py:369

commit v3 on v2

--- a/solution.py
+++ b/solution.py
@@ -70,8 +70,12 @@
     p_out,
     u_out,
     h_out,
-    main,
-    extra,
+    main_p,
+    main_u,
+    main_h,
+    extra_p,
+    extra_u,
+    extra_h,
     halo,
     first,
     second,
@@ -91,6 +95,8 @@
 ):
     fields = (p_in, u_in, h_in)
     outs = (p_out, u_out, h_out)
+    main = (main_p, main_u, main_h)
+    extra = (extra_p, extra_u, extra_h)
     s = lax.axis_index("slab")
     b = lax.axis_index("bal")
     ob = 1 - b
@@ -134,9 +140,9 @@
     for f in range(3):
         for j in range(2):
             t, i = edge_row(ob, j)
-            other_core(fields[f].at[:, t, :, i], extra.at[f, j, mine], 1).start()
+            other_core(fields[f].at[:, t, :, i], extra[f].at[j, mine], 3 + f).start()
         for c in range(8):
-            other_core(fields[f].at[:, theirs, c], main.at[f, mine, :, :, c], 0).start()
+            other_core(fields[f].at[:, theirs, c], main[f].at[mine, :, :, c], f).start()
 
     def to_layer(side, target):
         for f in range(3):
@@ -163,11 +169,11 @@
         for j in range(2):
             t, i = edge_row(b, j)
             pltpu.make_async_copy(
-                fields[f].at[:, t, :, i], extra.at[f, j, mine], local_sem.at[1]
+                fields[f].at[:, t, :, i], extra[f].at[j, mine], local_sem.at[3 + f]
             ).start()
         for c in range(8):
             pltpu.make_async_copy(
-                fields[f].at[:, mine, c], main.at[f, mine, :, :, c], local_sem.at[0]
+                fields[f].at[:, mine, c], main[f].at[mine, :, :, c], local_sem.at[f]
             ).start()
 
     for t in tables:
@@ -205,15 +211,13 @@
         for r in range(4):
             first[f, u, r] = planes[r]
 
-    def gather_extra(j):
-        for f in range(3):
-            keep(j, chunk_swap([extra[f, j, slot_here[p]] for p in range(4)], lane_block), f)
-
-    def gather(t, i):
+    def gather_extra(f, j):
+        keep(j, chunk_swap([extra[f][j, slot_here[p]] for p in range(4)], lane_block), f)
+
+    def gather(f, t, i):
         tile, row = place(t, i)
-        for f in range(3):
-            planes = [main[f, slot_here[p], tile, row] for p in range(4)]
-            keep(2 + 8 * t + i, chunk_swap(planes, lane_block), f)
+        planes = [main[f][slot_here[p], tile, row] for p in range(4)]
+        keep(2 + 8 * t + i, chunk_swap(planes, lane_block), f)
 
     def gather_halo(j):
         for f in range(3):
@@ -262,18 +266,18 @@
             ref, ref, side_send.at[side], side_recv, device_id=(s, ob), device_id_type=MESH
         )
 
-    pltpu.make_async_copy(main.at[:, mine], main.at[:, mine], local_sem.at[0]).wait()
-    pltpu.make_async_copy(extra.at[:, :, mine], extra.at[:, :, mine], local_sem.at[1]).wait()
-    other_core(extra.at[:, :, mine], extra.at[:, :, theirs], 1).wait_recv()
-    other_core(main.at[:, mine], main.at[:, theirs], 0).wait_recv()
-    def gather_tile(t, carry):
-        for i in range(8):
-            gather(t, i)
-        return carry
-
-    lax.fori_loop(0, 2, gather_tile, 0)
-    for j in range(2):
-        gather_extra(j)
+    for f in range(3):
+        own = main[f].at[mine]
+        own_edge = extra[f].at[:, mine]
+        pltpu.make_async_copy(own, own, local_sem.at[f]).wait()
+        pltpu.make_async_copy(own_edge, own_edge, local_sem.at[3 + f]).wait()
+        other_core(own_edge, extra[f].at[:, theirs], 3 + f).wait_recv()
+        other_core(own, main[f].at[theirs], f).wait_recv()
+
+        for t in range(2):
+            gather_extra(f, t)
+            for i in range(8):
+                gather(f, t, i)
 
     @pl.when(jnp.logical_not(at_wall))
     def _():
@@ -281,12 +285,13 @@
 
     for j in range(2):
         gather_halo(j)
+
     def step_rows(n, carry):
-        for i in range(6):
-            step_one(1 + 6 * n + i)
+        for i in range(9):
+            step_one(1 + 9 * n + i)
         return carry
 
-    lax.fori_loop(0, 3, step_rows, 0)
+    lax.fori_loop(0, 2, step_rows, 0)
     for f in range(3):
         for r in range(4):
             second[f, 18, r] = jnp.where(at_wall, second[f, 17, r], second[f, 18, r])
@@ -303,8 +308,9 @@
 
     lax.fori_loop(0, 4, finish, 0)
 
-    other_core(main.at[:, mine], main.at[:, theirs], 0).wait_send()
-    other_core(extra.at[:, :, mine], extra.at[:, :, theirs], 1).wait_send()
+    for f in range(3):
+        other_core(main[f].at[mine], main[f].at[theirs], f).wait_send()
+        other_core(extra[f].at[:, mine], extra[f].at[:, theirs], 3 + f).wait_send()
 
     @pl.when(has_high)
     def _():
@@ -342,8 +348,8 @@
         in_specs=[hbm] * 6,
         out_specs=(vmem,) * 3,
         scratch_shapes=[
-            pltpu.VMEM((3, 4, 2, 8, 8, 128), F32),
-            pltpu.VMEM((3, 2, 4, 8, 128), F32),
+            *[pltpu.VMEM((4, 2, 8, 8, 128), F32)] * 3,
+            *[pltpu.VMEM((2, 4, 8, 128), F32)] * 3,
             pltpu.VMEM((2, 3, 2, 2, 8, 128), F32),
             pltpu.VMEM((3, 20, 4, 8, 128), F32),
             pltpu.VMEM((3, 20, 4, 8, 128), F32),
@@ -353,9 +359,9 @@
             table,
             table,
             dma((3,)),
-            dma((2,)),
-            dma((2,)),
-            dma((2,)),
+            dma((6,)),
+            dma((6,)),
+            dma((6,)),
             dma((2,)),
             dma,
             dma((4, 3)),

time: 22.9 us -> 22.5 us (0.983)
  Pallas kernels: 22 us -> 21.5 us
    pallas_call x1, Pallas kernels: 21.1 us -> 20.6 us  [body(): pl.pallas_call(functools.partial(kernel, slabs), out_shape=(block,) * 3,...]
where the time goes in v3:
time: 22.5 us; the launch traced here: 22.2 us
  Pallas kernels  21.5 us (96%)
  between operations  0.64 us (3%)
    pallas_call x1, Pallas kernels, body(): pl.pallas_call(functools.partial(kernel, slabs), out_shape=(block,) * 3,...  20.6 us
    pallas_call x1, Pallas kernels, body(): pl.pallas_call(deliver, out_shape=(block,) * 3, in_specs=[anywhere] * 3,...  0.89 us

profile of v3, /device:TPU:1, one launch (start us, length us, event | category | flops | bytes accessed | tf_op | source)
XLA Modules:
  0.0 22.2 jit_solution(3206180906826510729)
XLA Ops:
  0.6 20.6 %sweeps.1 = (f32[2,4,8,8,128]{4,3,2,1,0:T(8,128)S(1)}, f32[2,4,8,8,128]{4,3,2,1,0:T(8,128)S(1)}, f32[2,4,8,8,128]{4,3,2,1,0:T(8,128)S(1)}) custom-call(f32[2,4,8,8,128]{4,3,2,1,0:T(8,128)} %bitcast.21, f32[2,4,8,8,128]{4,3,2,1,0:T(8,128)} %bitcast.22, f32[2,4,8,8,128]{4,3,2,1,0:T(8,128)} %bitcast.23, s32[4,512]{1,0:T(4,128)} %bitcast.24, s32[4,512]{1,0:T(4,128)} %bitcast.25, ...), custom_call_target="tpu_custom_call" | custom-call | tf_op jit(solution)/shard_map/sweeps/pallas_call | solution.py:345
  21.3 0.9 %deliver.1 = (f32[2,4,8,8,128]{4,3,2,1,0:T(8,128)}, f32[2,4,8,8,128]{4,3,2,1,0:T(8,128)}, f32[2,4,8,8,128]{4,3,2,1,0:T(8,128)}) custom-call(f32[2,4,8,8,128]{4,3,2,1,0:T(8,128)S(1)} %get-tuple-element.9.p_in, f32[2,4,8,8,128]{4,3,2,1,0:T(8,128)S(1)} %get-tuple-element.10.u_in, f32[2,4,8,8,128]{4,3,2,1,0:T(8,128)S(1)} %get-tuple-element.11.h_in), custom_call_target="tpu_custom_call" | custom-call | tf_op jit(solution)/shard_map/deliver/pallas_call | solution.py:375
